TPU v7x, 32 devices: a whole 2x2x4 slice. The times are simulated.
32 devices in a mesh: grp: 2 (over x), gx: 16 (over z, y, core).
Axes of the slice: x: 2, y: 2, z: 4, core: 2. Of those that a mesh axis runs over, the one named last changes fastest.
Arguments:
- grain_ids: int32 [96, 32, 512], P(('grp', 'gx')), parts along dimension 0, may hold values from 0 to 7
- jitter: bfloat16 [8, 96, 32, 512], P(None, ('grp', 'gx')), parts along dimension 1, may hold values from 0 to 0.5
- class_table: int32 [8, 8], replicated, may hold values from 0 to 3
- chosen: int32 [2], replicated, may hold values from 0 to 7
Outputs:
- order_params: float32 [8, 96, 32, 512], P(None, ('grp', 'gx')), parts along dimension 1
- correlation: float32 [2, 96, 32, 512], P(None, ('grp', 'gx')), parts along dimension 1
There are 2 independent parts, one for each index of `grp`. A program takes and returns all parts, laid end to end along the dimension named above; an argument that names none is the same for every part. Nothing has to cross between parts.
All inputs are finite; a program needn't handle non-finite values.
Results may differ from a plain program's by a relative error of at most 0.0003.
Values sent between devices are 32-bit elements; how exact they have to be, the bound alone decides.
No kernel may reach another device: no remote copies, remote signals or barrier semaphores. Data moves between devices by JAX's collectives and lax.ppermute only.
A program may use at most 128 MiB of HBM per device.

v0:
```python
import math
import jax
import jax.numpy as jnp
from jax import lax
from jax.sharding import PartitionSpec as P

STEPS = 3
HIGH = lax.Precision.HIGHEST


def with_halo(value, sides, width):
    for axis, dim in sides:
        peers, length = (lax.axis_size(axis), value.shape[dim])
        up = [(i, (i + 1) % peers) for i in range(peers)]
        down = [(j, i) for i, j in up]
        last = lax.slice_in_dim(value, length - width, length, axis=dim)
        initial = lax.slice_in_dim(value, 0, width, axis=dim)
        before = lax.ppermute(last, axis, up)
        after = lax.ppermute(initial, axis, down)
        value = jnp.concatenate([before, value, after], axis=dim)
    return value


def tables(length):
    index = lax.iota(jnp.int32, length)
    product = index[:, None] * index[None, :] % length
    angle = product.astype(jnp.float32) * (2.0 * math.pi / length)
    return (jnp.cos(angle), jnp.sin(angle))


def onehot_of(grain_ids):
    return (grain_ids[None] == lax.iota(jnp.int32, 8)[:, None, None, None]).astype(jnp.float32)


def levels_map(onehot, class_table):
    levels = 0.4 + 0.2 * class_table.astype(jnp.float32)
    return jnp.einsum("gi,gxzy->ixzy", levels, onehot, precision=HIGH)


def advance(extended, mobility):
    center = extended[:, 1:-1]
    lap = extended[:, 2:] + extended[:, :-2]
    lap = lap + jnp.roll(center, -1, 2) + jnp.roll(center, 1, 2)
    lap = lap + jnp.roll(center, -1, 3) + jnp.roll(center, 1, 3)
    lap = lap - 6.0 * center
    total = jnp.sum(center * center, axis=0)
    drive = -center + center * center * center + 3.0 * center * (total[None] - center * center)
    return center - 0.12 * mobility * (drive - lap)


def forward_planes(fields, cos_y, sin_y, cos_z, sin_z):
    real_y = jnp.dot(fields, cos_y, precision=HIGH)
    imag_y = -jnp.dot(fields, sin_y, precision=HIGH)
    real_z = jnp.einsum("kz,fxzy->fxky", cos_z, real_y, precision=HIGH) + jnp.einsum(
        "kz,fxzy->fxky", sin_z, imag_y, precision=HIGH
    )
    imag_z = jnp.einsum("kz,fxzy->fxky", cos_z, imag_y, precision=HIGH) - jnp.einsum(
        "kz,fxzy->fxky", sin_z, real_y, precision=HIGH
    )
    planes = fields.shape[1]
    return (
        real_z.reshape(fields.shape[0], planes, -1),
        imag_z.reshape(fields.shape[0], planes, -1),
    )


def line_power(real_part, imag_part, cos_x, sin_x, offset):
    real_x = jnp.einsum("kx,fxc->fkc", cos_x, real_part, precision=HIGH) + jnp.einsum(
        "kx,fxc->fkc", sin_x, imag_part, precision=HIGH
    )
    imag_x = jnp.einsum("kx,fxc->fkc", cos_x, imag_part, precision=HIGH) - jnp.einsum(
        "kx,fxc->fkc", sin_x, real_part, precision=HIGH
    )
    power = real_x * real_x + imag_x * imag_x
    freq_x = lax.iota(jnp.int32, power.shape[1])[:, None]
    column = offset + lax.iota(jnp.int32, power.shape[2])[None, :]
    keep = jnp.logical_not(jnp.logical_and(freq_x == 0, column == 0))
    power = power * keep.astype(jnp.float32)[None]
    back_real = jnp.einsum("kx,fkc->fxc", cos_x, power, precision=HIGH)
    back_imag = jnp.einsum("kx,fkc->fxc", sin_x, power, precision=HIGH)
    return (back_real, back_imag)


def inverse_planes(back_real, back_imag, cos_y, sin_y, cos_z, sin_z, depth, width, count):
    fields = back_real.shape[0]
    planes = back_real.shape[1]
    back_real = back_real.reshape(fields, planes, depth, width)
    back_imag = back_imag.reshape(fields, planes, depth, width)
    real_z = jnp.einsum("kz,fxky->fxzy", cos_z, back_real, precision=HIGH) - jnp.einsum(
        "kz,fxky->fxzy", sin_z, back_imag, precision=HIGH
    )
    imag_z = jnp.einsum("kz,fxky->fxzy", cos_z, back_imag, precision=HIGH) + jnp.einsum(
        "kz,fxky->fxzy", sin_z, back_real, precision=HIGH
    )
    result = jnp.dot(real_z, cos_y, precision=HIGH) - jnp.dot(imag_z, sin_y, precision=HIGH)
    return result / (count * count)


def shards(grain_ids, jitter, class_table, chosen):
    planes = grain_ids.shape[0]
    depth = grain_ids.shape[1]
    width = grain_ids.shape[2]
    devices = lax.axis_size("gx")
    onehot = onehot_of(grain_ids)
    eta = 0.6 * onehot + jitter.astype(jnp.float32)
    mobility = levels_map(onehot, class_table)
    for step in range(STEPS):
        extended = with_halo(eta, (("gx", 1),), 1)
        eta = advance(extended, mobility)
    select = (chosen[:, None] == lax.iota(jnp.int32, 8)[None, :]).astype(jnp.float32)
    fields = jnp.einsum("ki,ixzy->kxzy", select, eta, precision=HIGH)
    cos_y, sin_y = tables(width)
    cos_z, sin_z = tables(depth)
    total_x = planes * devices
    cos_x, sin_x = tables(total_x)
    count = float(total_x * depth * width)
    columns = depth * width // devices
    offset = lax.axis_index("gx") * columns
    real_part, imag_part = forward_planes(fields, cos_y, sin_y, cos_z, sin_z)
    stacked = jnp.concatenate([real_part, imag_part], axis=0)
    lines = lax.all_to_all(stacked, "gx", split_axis=2, concat_axis=1, tiled=True)
    back_real, back_imag = line_power(lines[:2], lines[2:], cos_x, sin_x, offset)
    returned = lax.all_to_all(
        jnp.concatenate([back_real, back_imag], axis=0),
        "gx",
        split_axis=1,
        concat_axis=2,
        tiled=True,
    )
    correlation = inverse_planes(
        returned[:2], returned[2:], cos_y, sin_y, cos_z, sin_z, depth, width, count
    )
    return (eta, correlation)


def solution(mesh):
    in_specs = (P(("grp", "gx"), None, None), P(None, ("grp", "gx"), None, None), P(), P())
    out_specs = (P(None, ("grp", "gx"), None, None), P(None, ("grp", "gx"), None, None))
    return jax.shard_map(shards, mesh=mesh, in_specs=in_specs, out_specs=out_specs, check_vma=False)
```

profile of v0, /device:TPU:11, one launch (start us, length us, event | category | flops | bytes accessed | tf_op | source)
XLA Modules:
  0.0 307.3 jit_solution(3220175203014402098)
XLA Ops:
  0.6 1.8 convert_add_fusion
  5.1 14.7 %multiply_subtract_fusion.2 = f32[8,3,32,512]{3,0,2,1:T(8,128)S(1)} fusion(bf16[8,3,32,512]{3,2,1,0:T(8,128)(2,1)S(1)} %copy-done.1, s32[3,32,512]{2,1,0:T(8,128)S(1)} %copy-done), kind=kOutput, calls=%fused_computation.12 | output fusion | flops 4374535 | bytes 2555904 | tf_op jit(solution)/shard_map/sub | solution.py:47
  20.6 2.2 fusion.16
  23.7 1.6 collective-permute-start.3
  25.9 11.9 %collective-permute-done.2 = f32[8,1,32,512]{3,0,2,1:T(8,128)S(1)} collective-permute-done((f32[8,1,32,512]{3,0,2,1:T(8,128)S(1)}, f32[8,1,32,512]{3,0,2,1:T(8,128)S(1)}, u32[]{:S(2)}, u32[]{:S(2)}) %collective-permute-start.2) | collective-permute-done | bytes 524320 | tf_op jit(solution)/shard_map/ppermute | solution.py:19
  37.8 34.6 %fusion.21 = f32[8,3,32,512]{3,0,2,1:T(8,128)S(1)} fusion(f32[8,3,32,512]{3,0,2,1:T(8,128)S(1)} %get-tuple-element.42, f32[8,3,32,512]{3,0,2,1:T(8,128)S(1)} %get-tuple-element.43, f32[8,1,32,512]{3,0,2,1:T(8,128)S(1)} %collective-permute-done.3, f32[8,1,32,512]{3,0,2,1:T(8,128)S(1)} %collective-permute-done.2, f32[8,3,1,512]{3,0,2,1:T(8,128)S(1)} %get-tuple-element.23, ...), kind=kOutput, calls=%fused_computation.24 | output fusion | flops 9879559 | bytes 12058624 | tf_op jit(solution)/shard_map/sub | solution.py:47
  73.2 2.3 collective-permute-start.5
  76.0 11.4 %collective-permute-done.4 = f32[8,1,32,512]{3,0,2,1:T(8,128)S(1)} collective-permute-done((f32[8,1,32,512]{3,0,2,1:T(8,128)S(1)}, f32[8,1,32,512]{3,0,2,1:T(8,128)S(1)}, u32[]{:S(2)}, u32[]{:S(2)}) %collective-permute-start.4) | collective-permute-done | bytes 524320 | tf_op jit(solution)/shard_map/ppermute | solution.py:19
  87.4 34.6 %fusion.26 = f32[8,3,32,512]{3,0,2,1:T(8,128)S(1)} fusion(f32[8,3,32,512]{3,0,2,1:T(8,128)S(1)} %fusion.21, f32[8,3,32,512]{3,0,2,1:T(8,128)S(1)} %get-tuple-element.43, f32[8,1,32,512]{3,0,2,1:T(8,128)S(1)} %collective-permute-done.5, f32[8,1,32,512]{3,0,2,1:T(8,128)S(1)} %collective-permute-done.4, f32[8,3,1,512]{3,0,2,1:T(8,128)S(1)} %get-tuple-element.13, ...), kind=kOutput, calls=%fused_computation.29 | output fusion | flops 9879559 | bytes 12058624 | tf_op jit(solution)/shard_map/sub | solution.py:47
  122.9 5.1 %fusion.62 = f32[2,3,32,512]{3,2,1,0:T(8,128)S(1)} fusion(f32[2,3,32,512]{3,0,2,1:T(2,128)S(1)} %fusion.155), kind=kOutput, calls=%fused_computation.86 | convolution fusion | flops 607649792 | bytes 786432 | tf_op jit(solution)/shard_map/dot_general | solution.py:52
  128.1 5.1 %convolution_negate_fusion = f32[2,3,32,512]{3,2,1,0:T(8,128)S(1)} fusion(f32[2,3,32,512]{3,0,2,1:T(2,128)S(1)} %fusion.155), kind=kOutput, calls=%fused_computation.76 | convolution fusion | flops 607748096 | bytes 786432 | tf_op jit(solution)/shard_map/dot_general | solution.py:53
  136.7 20.3 %copy.46 = f32[4,3,16384]{0,1,2:T(4,128)} copy(f32[4,3,16384]{2,0,1:T(4,128)S(1)} %pad_maximum_fusion.6) | data formatting | bytes 1572864 | tf_op jit(solution)/shard_map/concatenate | solution.py:120
  157.0 24.8 %reshape.88 = f32[16,1,12288]{2,1,0:T(1,128)} reshape(f32[16384,3,4]{2,1,0:T(4,128)} %bitcast.118) | data formatting | bytes 1572864
  181.8 7.3 %all-to-all-start = ((f32[16,1,12288]{2,1,0:T(1,128)}), f32[16,1,12288]{2,1,0:T(1,128)S(1)}, u32[]{:S(2)}, u32[]{:S(2)}) async-start(f32[16,1,12288]{2,1,0:T(1,128)} %reshape.88), calls=%async_computation | async-start | bytes 1572864 | tf_op jit(solution)/shard_map/all_to_all | solution.py:121
  189.3 19.3 %all-to-all-done = f32[16,1,12288]{2,1,0:T(1,128)S(1)} async-done(((f32[16,1,12288]{2,1,0:T(1,128)}), f32[16,1,12288]{2,1,0:T(1,128)S(1)}, u32[]{:S(2)}, u32[]{:S(2)}) %all-to-all-start) | async-done | bytes 786464 | tf_op jit(solution)/shard_map/all_to_all | solution.py:121
  209.1 2.5 reduce
  211.6 33.0 %reshape.89 = f32[16384,3,4]{2,1,0:T(4,128)} reshape(f32[16,12288]{1,0:T(8,128)S(1)} %reduce) | data formatting | bytes 1572864
  244.7 18.5 %copy.81 = f32[4,3,16,1024]{3,2,0,1:T(8,128)S(1)} copy(f32[4,3,16,1024]{0,1,3,2:T(4,128)} %bitcast.119) | data formatting | bytes 1572864 | tf_op jit(solution)/shard_map/all_to_all | solution.py:121
  267.9 1.4 copy.58
  269.3 4.6 %all-to-all-start.1 = ((f32[4,48,1024]{2,0,1:T(4,128)}), f32[4,48,1024]{2,0,1:T(4,128)S(1)}, u32[]{:S(2)}, u32[]{:S(2)}) async-start(f32[4,48,1024]{2,0,1:T(4,128)} %copy.58), calls=%async_computation.1 | async-start | bytes 1572864 | tf_op jit(solution)/shard_map/all_to_all | solution.py:123
  273.9 2.1 copy.61
  276.0 17.5 %all-to-all-done.1 = f32[4,48,1024]{2,0,1:T(4,128)S(1)} async-done(((f32[4,48,1024]{2,0,1:T(4,128)}), f32[4,48,1024]{2,0,1:T(4,128)S(1)}, u32[]{:S(2)}, u32[]{:S(2)}) %all-to-all-start.1) | async-done | bytes 786464 | tf_op jit(solution)/shard_map/all_to_all | solution.py:123
  296.4 5.1 %fusion.60 = f32[2,3,32,512]{3,2,1,0:T(8,128)S(1)} fusion(f32[2,3,32,512]{3,2,1,0:T(8,128)S(1)} %fusion.48), kind=kOutput, calls=%fused_computation.84 | convolution fusion | flops 607649792 | bytes 786432 | tf_op jit(solution)/shard_map/dot_general | solution.py:95
  301.5 5.6 %fusion.56 = f32[2,3,32,512]{3,2,1,0:T(8,128)} fusion(f32[2,3,32,512]{3,2,1,0:T(8,128)S(1)} %fusion.60, f32[2,3,32,512]{3,2,1,0:T(8,128)S(1)} %fusion.47), kind=kOutput, calls=%fused_computation.80 | convolution fusion | flops 607846400 | bytes 1179648 | tf_op jit(solution)/shard_map/dot_general | solution.py:95
  (64 shorter events, 18.5 us)
Async XLA Ops:
  2.5 17.9 %collective-permute-start = (f32[8,1,32,512]{3,0,2,1:T(8,128)S(1)}, f32[8,1,32,512]{3,0,2,1:T(8,128)S(1)}, u32[]{:S(2)}, u32[]{:S(2)}) collective-permute-start(f32[8,1,32,512]{3,0,2,1:T(8,128)S(1)} %get-tuple-element.36), channel_id=1, source_target_pairs={{1,0},{2,1},{3,2},{4,3},{5,4},{6,5},{7,6},{8,7},{9,8},{10,9},{11,1... | collective-permute-start | bytes 1572872 | tf_op jit(solution)/shard_map/ppermute | solution.py:19
  3.2 1.8 copy-start
  3.2 1.8 copy-start.1
  3.3 17.2 %collective-permute-start.1 = (f32[8,1,32,512]{3,0,2,1:T(8,128)S(1)}, f32[8,1,32,512]{3,0,2,1:T(8,128)S(1)}, u32[]{:S(2)}, u32[]{:S(2)}) collective-permute-start(f32[8,1,32,512]{3,0,2,1:T(8,128)S(1)} %get-tuple-element.37), channel_id=1, source_target_pairs={{0,1},{1,2},{2,3},{3,4},{4,5},{5,6},{6,7},{7,8},{8,9},{9,10},{10,1... | collective-permute-start | bytes 1572872 | tf_op jit(solution)/shard_map/ppermute | solution.py:18
  19.9 0.7 copy-start.2
  23.5 14.3 %collective-permute-start.2 = (f32[8,1,32,512]{3,0,2,1:T(8,128)S(1)}, f32[8,1,32,512]{3,0,2,1:T(8,128)S(1)}, u32[]{:S(2)}, u32[]{:S(2)}) collective-permute-start(f32[8,1,32,512]{3,0,2,1:T(8,128)S(1)} %get-tuple-element.26), channel_id=1, source_target_pairs={{1,0},{2,1},{3,2},{4,3},{5,4},{6,5},{7,6},{8,7},{9,8},{10,9},{11,1... | collective-permute-start | bytes 1572872 | tf_op jit(solution)/shard_map/ppermute | solution.py:19
  23.7 14.1 %collective-permute-start.3 = (f32[8,1,32,512]{3,0,2,1:T(8,128)S(1)}, f32[8,1,32,512]{3,0,2,1:T(8,128)S(1)}, u32[]{:S(2)}, u32[]{:S(2)}) collective-permute-start(f32[8,1,32,512]{3,0,2,1:T(8,128)S(1)} %get-tuple-element.27), channel_id=1, source_target_pairs={{0,1},{1,2},{2,3},{3,4},{4,5},{5,6},{6,7},{7,8},{8,9},{9,10},{10,1... | collective-permute-start | bytes 1572872 | tf_op jit(solution)/shard_map/ppermute | solution.py:18
  73.1 14.3 %collective-permute-start.4 = (f32[8,1,32,512]{3,0,2,1:T(8,128)S(1)}, f32[8,1,32,512]{3,0,2,1:T(8,128)S(1)}, u32[]{:S(2)}, u32[]{:S(2)}) collective-permute-start(f32[8,1,32,512]{3,0,2,1:T(8,128)S(1)} %get-tuple-element.16), channel_id=1, source_target_pairs={{1,0},{2,1},{3,2},{4,3},{5,4},{6,5},{7,6},{8,7},{9,8},{10,9},{11,1... | collective-permute-start | bytes 1572872 | tf_op jit(solution)/shard_map/ppermute | solution.py:19
  73.2 14.2 %collective-permute-start.5 = (f32[8,1,32,512]{3,0,2,1:T(8,128)S(1)}, f32[8,1,32,512]{3,0,2,1:T(8,128)S(1)}, u32[]{:S(2)}, u32[]{:S(2)}) collective-permute-start(f32[8,1,32,512]{3,0,2,1:T(8,128)S(1)} %get-tuple-element.17), channel_id=1, source_target_pairs={{0,1},{1,2},{2,3},{3,4},{4,5},{5,6},{6,7},{7,8},{8,9},{9,10},{10,1... | collective-permute-start | bytes 1572872 | tf_op jit(solution)/shard_map/ppermute | solution.py:18
  87.4 34.7 %copy-start.3 = (s32[2]{0:T(128)S(1)}, s32[2]{0:T(128)}, u32[]{:S(2)}) copy-start(s32[2]{0:T(128)} %param.7) | copy-start | bytes 28
  181.8 26.8 %all-to-all-start = ((f32[16,1,12288]{2,1,0:T(1,128)}), f32[16,1,12288]{2,1,0:T(1,128)S(1)}, u32[]{:S(2)}, u32[]{:S(2)}) async-start(f32[16,1,12288]{2,1,0:T(1,128)} %reshape.88), calls=%async_computation | async-start | bytes 1572864 | tf_op jit(solution)/shard_map/all_to_all | solution.py:121
  269.3 24.2 %all-to-all-start.1 = ((f32[4,48,1024]{2,0,1:T(4,128)}), f32[4,48,1024]{2,0,1:T(4,128)S(1)}, u32[]{:S(2)}, u32[]{:S(2)}) async-start(f32[4,48,1024]{2,0,1:T(4,128)} %copy.58), calls=%async_computation.1 | async-start | bytes 1572864 | tf_op jit(solution)/shard_map/all_to_all | solution.py:123
where the time goes:
time: 313 us; the launch traced here: 307 us
  local copies, waits for them, and re-layouts  107 us (34%)
  other arithmetic  88.9 us (28%)
  waiting for transfers between devices  60.1 us (19%)
  matrix products  32.5 us (10%)
  starting transfers between devices  18 us (6%)
    sub x3, other arithmetic, advance(): total[None] - center * center  84 us
    unnamed x11, local copies, waits for them, and re-layouts  60 us
    ppermute x3, waiting for transfers between devices, with_halo(): after = lax.ppermute(initial, axis, down)  23.3 us
    concatenate x1, local copies, waits for them, and re-layouts, shards(): stacked = jnp.concatenate([real_part, imag_part], axis=0)  20.3 us
    all_to_all x1, waiting for transfers between devices, shards(): lax.all_to_all(stacked, 'gx', split_axis=2, concat_axis=1, tiled=True)  19.3 us
    all_to_all x2, local copies, waits for them, and re-layouts, shards(): lax.all_to_all(stacked, 'gx', split_axis=2, concat_axis=1, tiled=True)  19 us
    all_to_all x1, waiting for transfers between devices, shards(): lax.all_to_all(jnp.concatenate([back_real, back_imag], axis=0), 'gx', spl...  17.5 us
    all_to_all x1, starting transfers between devices, shards(): lax.all_to_all(stacked, 'gx', split_axis=2, concat_axis=1, tiled=True)  7.34 us
  transfers between devices with their start and end apart: 8, of which 4 were waited for; matrix products, arithmetic and copies ran while one was open for 6% of the time, Pallas kernels for 0%

commit v1 on v0

--- a/solution.py
+++ b/solution.py
@@ -118,7 +118,10 @@
     offset = lax.axis_index("gx") * columns
     real_part, imag_part = forward_planes(fields, cos_y, sin_y, cos_z, sin_z)
     stacked = jnp.concatenate([real_part, imag_part], axis=0)
-    lines = lax.all_to_all(stacked, "gx", split_axis=2, concat_axis=1, tiled=True)
+    lines = jnp.concatenate(
+        lax.all_to_all(jnp.stack(jnp.split(stacked, lax.axis_size("gx"), axis=2)), "gx", 0, 0),
+        axis=1,
+    )
     back_real, back_imag = line_power(lines[:2], lines[2:], cos_x, sin_x, offset)
     returned = lax.all_to_all(
         jnp.concatenate([back_real, back_imag], axis=0),

time: 313 us -> 218 us (0.70); the launches traced: 307 us -> 217 us
  local copies, waits for them, and re-layouts: 107 us -> 10 us
  other arithmetic: 88.9 us -> 96.2 us
    unnamed x11 -> x9, local copies, waits for them, and re-layouts: 60 us -> 3.19 us
    concatenate x1 -> x0, local copies, waits for them, and re-layouts: 20.3 us -> none  [shards(): stacked = jnp.concatenate([real_part, imag_part], axis=0)]
    all_to_all x2 -> x0, local copies, waits for them, and re-layouts: 19 us -> none  [shards(): lax.all_to_all(stacked, 'gx', split_axis=2, concat_axis=1, tiled=True)]
    unnamed x0 -> x15, other arithmetic: none -> 9.66 us
  transfers between devices with their start and end apart: 8 -> 8, of which waited for: 4 -> 4; matrix products, arithmetic and copies ran while one was open for 6% -> 9% of each run, Pallas kernels for 0% -> 0%
where the time goes in v1:
time: 218 us; the launch traced here: 217 us
  other arithmetic  96.2 us (44%)
  waiting for transfers between devices  60.5 us (28%)
  matrix products  32.5 us (15%)
  starting transfers between devices  17.2 us (8%)
  local copies, waits for them, and re-layouts  10 us (5%)
    sub x3, other arithmetic, advance(): total[None] - center * center  83.9 us
    ppermute x3, waiting for transfers between devices, with_halo(): after = lax.ppermute(initial, axis, down)  23.5 us
    all_to_all x1, waiting for transfers between devices, shards(): lax.all_to_all(jnp.stack(jnp.split(stacked, lax.axis_size('gx'), axis=2))...  19.4 us
    all_to_all x1, waiting for transfers between devices, shards(): lax.all_to_all(jnp.concatenate([back_real, back_imag], axis=0), 'gx', spl...  17.5 us
    unnamed x15, other arithmetic  9.66 us
    all_to_all x1, starting transfers between devices, shards(): lax.all_to_all(jnp.stack(jnp.split(stacked, lax.axis_size('gx'), axis=2))...  6.8 us
    dot_general x1, matrix products, inverse_planes(): jnp.dot(imag_z, sin_y, precision=HIGH)  5.6 us
    dot_general x1, matrix products, forward_planes(): real_y = jnp.dot(fields, cos_y, precision=HIGH)  5.12 us
  transfers between devices with their start and end apart: 8, of which 4 were waited for; matrix products, arithmetic and copies ran while one was open for 9% of the time, Pallas kernels for 0%

profile of v1, /device:TPU:11, one launch (start us, length us, event | category | flops | bytes accessed | tf_op | source)
XLA Modules:
  0.0 217.4 jit_solution(7832977143620745758)
XLA Ops:
  0.6 1.8 convert_add_fusion
  2.5 0.7 collective-permute-start
  3.2 1.2 collective-permute-start.1
  5.1 0.7 copy-done
  6.1 14.6 %multiply_subtract_fusion.2 = f32[8,3,32,512]{3,0,2,1:T(8,128)S(1)} fusion(bf16[8,3,32,512]{3,2,1,0:T(8,128)(2,1)S(1)} %copy-done.1, s32[3,32,512]{2,1,0:T(8,128)S(1)} %copy-done), kind=kOutput, calls=%fused_computation.42 | output fusion | flops 4374535 | bytes 2555904 | tf_op jit(solution)/shard_map/sub | solution.py:47
  21.5 2.2 %fusion.16 = (f32[8,3,32,512]{3,0,2,1:T(8,128)S(1)}, f32[8,3,32,512]{3,0,2,1:T(8,128)S(1)}) fusion(f32[8,3,32,512]{3,0,2,1:T(8,128)S(1)} %convert_add_fusion, f32[8,1,32,512]{3,0,2,1:T(8,128)S(1)} %collective-permute-done.1, f32[8,1,32,512]{3,0,2,1:T(8,128)S(1)} %collective-permute-done, f32[8,3,1,512]{3,0,2,1:T(8,128)S(1)} %get-tuple-element.33, ...), kind=kOutput, calls=%fused_computation.49 | convolution fusion | flops 47579328 | bytes 13828352 | tf_op jit(solution)/shard_map/gi,gxzy->ixzy/dot_general | solution.py:37
  24.4 1.7 collective-permute-start.3
  26.8 11.9 %collective-permute-done.2 = f32[8,1,32,512]{3,0,2,1:T(8,128)S(1)} collective-permute-done((f32[8,1,32,512]{3,0,2,1:T(8,128)S(1)}, f32[8,1,32,512]{3,0,2,1:T(8,128)S(1)}, u32[]{:S(2)}, u32[]{:S(2)}) %collective-permute-start.2) | collective-permute-done | bytes 524320 | tf_op jit(solution)/shard_map/ppermute | solution.py:19
  38.7 34.6 %fusion.21 = f32[8,3,32,512]{3,0,2,1:T(8,128)S(1)} fusion(f32[8,3,32,512]{3,0,2,1:T(8,128)S(1)} %get-tuple-element.42, f32[8,3,32,512]{3,0,2,1:T(8,128)S(1)} %get-tuple-element.43, f32[8,1,32,512]{3,0,2,1:T(8,128)S(1)} %collective-permute-done.3, f32[8,1,32,512]{3,0,2,1:T(8,128)S(1)} %collective-permute-done.2, f32[8,3,1,512]{3,0,2,1:T(8,128)S(1)} %get-tuple-element.23, ...), kind=kOutput, calls=%fused_computation.54 | output fusion | flops 9879559 | bytes 12058624 | tf_op jit(solution)/shard_map/sub | solution.py:47
  74.1 2.0 collective-permute-start.5
  76.6 11.7 %collective-permute-done.4 = f32[8,1,32,512]{3,0,2,1:T(8,128)S(1)} collective-permute-done((f32[8,1,32,512]{3,0,2,1:T(8,128)S(1)}, f32[8,1,32,512]{3,0,2,1:T(8,128)S(1)}, u32[]{:S(2)}, u32[]{:S(2)}) %collective-permute-start.4) | collective-permute-done | bytes 524320 | tf_op jit(solution)/shard_map/ppermute | solution.py:19
  88.3 34.6 %fusion.26 = f32[8,3,32,512]{3,0,2,1:T(8,128)S(1)} fusion(f32[8,3,32,512]{3,0,2,1:T(8,128)S(1)} %fusion.21, f32[8,3,32,512]{3,0,2,1:T(8,128)S(1)} %get-tuple-element.43, f32[8,1,32,512]{3,0,2,1:T(8,128)S(1)} %collective-permute-done.5, f32[8,1,32,512]{3,0,2,1:T(8,128)S(1)} %collective-permute-done.4, f32[8,3,1,512]{3,0,2,1:T(8,128)S(1)} %get-tuple-element.13, ...), kind=kOutput, calls=%fused_computation.59 | output fusion | flops 9879559 | bytes 12058624 | tf_op jit(solution)/shard_map/sub | solution.py:47
  123.0 0.9 fusion.172
  123.8 5.1 %fusion.62 = f32[2,3,32,512]{3,2,1,0:T(8,128)S(1)} fusion(f32[2,3,32,512]{3,0,2,1:T(2,128)S(1)} %fusion.172), kind=kOutput, calls=%fused_computation.116 | convolution fusion | flops 607649792 | bytes 786432 | tf_op jit(solution)/shard_map/dot_general | solution.py:52
  129.0 5.1 %convolution_negate_fusion = f32[2,3,32,512]{3,2,1,0:T(8,128)S(1)} fusion(f32[2,3,32,512]{3,0,2,1:T(2,128)S(1)} %fusion.172), kind=kOutput, calls=%fused_computation.106 | convolution fusion | flops 607748096 | bytes 786432 | tf_op jit(solution)/shard_map/dot_general | solution.py:53
  147.5 6.8 %all-to-all-start = ((f32[16,4,3,1024]{3,1,2,0:T(4,128)}), f32[16,4,3,1024]{3,1,2,0:T(4,128)S(1)}, u32[]{:S(2)}, u32[]{:S(2)}) async-start(f32[16,4,3,1024]{3,1,2,0:T(4,128)} %fusion.100), calls=%async_computation | async-start | bytes 1572864 | tf_op jit(solution)/shard_map/all_to_all | solution.py:122
  154.5 19.4 %all-to-all-done = f32[16,4,3,1024]{3,1,2,0:T(4,128)S(1)} async-done(((f32[16,4,3,1024]{3,1,2,0:T(4,128)}), f32[16,4,3,1024]{3,1,2,0:T(4,128)S(1)}, u32[]{:S(2)}, u32[]{:S(2)}) %all-to-all-start) | async-done | bytes 786464 | tf_op jit(solution)/shard_map/all_to_all | solution.py:122
  176.2 0.7 fusion.55
  178.2 1.4 copy.53
  179.6 4.6 %all-to-all-start.1 = ((f32[4,48,1024]{2,0,1:T(4,128)}), f32[4,48,1024]{2,0,1:T(4,128)S(1)}, u32[]{:S(2)}, u32[]{:S(2)}) async-start(f32[4,48,1024]{2,0,1:T(4,128)} %copy.53), calls=%async_computation.1 | async-start | bytes 1572864 | tf_op jit(solution)/shard_map/all_to_all | solution.py:126
  184.3 2.1 copy.56
  186.3 17.5 %all-to-all-done.1 = f32[4,48,1024]{2,0,1:T(4,128)S(1)} async-done(((f32[4,48,1024]{2,0,1:T(4,128)}), f32[4,48,1024]{2,0,1:T(4,128)S(1)}, u32[]{:S(2)}, u32[]{:S(2)}) %all-to-all-start.1) | async-done | bytes 786464 | tf_op jit(solution)/shard_map/all_to_all | solution.py:126
  206.8 5.1 %fusion.60 = f32[2,3,32,512]{3,2,1,0:T(8,128)S(1)} fusion(f32[2,3,32,512]{3,2,1,0:T(8,128)S(1)} %fusion.48), kind=kOutput, calls=%fused_computation.114 | convolution fusion | flops 607649792 | bytes 786432 | tf_op jit(solution)/shard_map/dot_general | solution.py:95
  211.9 5.6 %fusion.56 = f32[2,3,32,512]{3,2,1,0:T(8,128)} fusion(f32[2,3,32,512]{3,2,1,0:T(8,128)S(1)} %fusion.60, f32[2,3,32,512]{3,2,1,0:T(8,128)S(1)} %fusion.47), kind=kOutput, calls=%fused_computation.110 | convolution fusion | flops 607846400 | bytes 1179648 | tf_op jit(solution)/shard_map/dot_general | solution.py:95
  (71 shorter events, 24.2 us)
Async XLA Ops:
  2.5 18.8 %collective-permute-start = (f32[8,1,32,512]{3,0,2,1:T(8,128)S(1)}, f32[8,1,32,512]{3,0,2,1:T(8,128)S(1)}, u32[]{:S(2)}, u32[]{:S(2)}) collective-permute-start(f32[8,1,32,512]{3,0,2,1:T(8,128)S(1)} %get-tuple-element.36), channel_id=1, source_target_pairs={{1,0},{2,1},{3,2},{4,3},{5,4},{6,5},{7,6},{8,7},{9,8},{10,9},{11,1... | collective-permute-start | bytes 1572872 | tf_op jit(solution)/shard_map/ppermute | solution.py:19
  3.2 18.1 %collective-permute-start.1 = (f32[8,1,32,512]{3,0,2,1:T(8,128)S(1)}, f32[8,1,32,512]{3,0,2,1:T(8,128)S(1)}, u32[]{:S(2)}, u32[]{:S(2)}) collective-permute-start(f32[8,1,32,512]{3,0,2,1:T(8,128)S(1)} %get-tuple-element.37), channel_id=1, source_target_pairs={{0,1},{1,2},{2,3},{3,4},{4,5},{5,6},{6,7},{7,8},{8,9},{9,10},{10,1... | collective-permute-start | bytes 1572872 | tf_op jit(solution)/shard_map/ppermute | solution.py:18
  4.9 0.9 copy-start
  4.9 1.2 copy-start.1
  20.8 0.7 copy-start.2
  24.4 14.3 %collective-permute-start.2 = (f32[8,1,32,512]{3,0,2,1:T(8,128)S(1)}, f32[8,1,32,512]{3,0,2,1:T(8,128)S(1)}, u32[]{:S(2)}, u32[]{:S(2)}) collective-permute-start(f32[8,1,32,512]{3,0,2,1:T(8,128)S(1)} %get-tuple-element.26), channel_id=1, source_target_pairs={{1,0},{2,1},{3,2},{4,3},{5,4},{6,5},{7,6},{8,7},{9,8},{10,9},{11,1... | collective-permute-start | bytes 1572872 | tf_op jit(solution)/shard_map/ppermute | solution.py:19
  24.4 14.2 %collective-permute-start.3 = (f32[8,1,32,512]{3,0,2,1:T(8,128)S(1)}, f32[8,1,32,512]{3,0,2,1:T(8,128)S(1)}, u32[]{:S(2)}, u32[]{:S(2)}) collective-permute-start(f32[8,1,32,512]{3,0,2,1:T(8,128)S(1)} %get-tuple-element.27), channel_id=1, source_target_pairs={{0,1},{1,2},{2,3},{3,4},{4,5},{5,6},{6,7},{7,8},{8,9},{9,10},{10,1... | collective-permute-start | bytes 1572872 | tf_op jit(solution)/shard_map/ppermute | solution.py:18
  74.0 14.3 %collective-permute-start.4 = (f32[8,1,32,512]{3,0,2,1:T(8,128)S(1)}, f32[8,1,32,512]{3,0,2,1:T(8,128)S(1)}, u32[]{:S(2)}, u32[]{:S(2)}) collective-permute-start(f32[8,1,32,512]{3,0,2,1:T(8,128)S(1)} %get-tuple-element.16), channel_id=1, source_target_pairs={{1,0},{2,1},{3,2},{4,3},{5,4},{6,5},{7,6},{8,7},{9,8},{10,9},{11,1... | collective-permute-start | bytes 1572872 | tf_op jit(solution)/shard_map/ppermute | solution.py:19
  74.1 14.2 %collective-permute-start.5 = (f32[8,1,32,512]{3,0,2,1:T(8,128)S(1)}, f32[8,1,32,512]{3,0,2,1:T(8,128)S(1)}, u32[]{:S(2)}, u32[]{:S(2)}) collective-permute-start(f32[8,1,32,512]{3,0,2,1:T(8,128)S(1)} %get-tuple-element.17), channel_id=1, source_target_pairs={{0,1},{1,2},{2,3},{3,4},{4,5},{5,6},{6,7},{7,8},{8,9},{9,10},{10,1... | collective-permute-start | bytes 1572872 | tf_op jit(solution)/shard_map/ppermute | solution.py:18
  88.3 34.7 %copy-start.3 = (s32[2]{0:T(128)S(1)}, s32[2]{0:T(128)}, u32[]{:S(2)}) copy-start(s32[2]{0:T(128)} %param.7) | copy-start | bytes 28
  147.5 26.4 %all-to-all-start = ((f32[16,4,3,1024]{3,1,2,0:T(4,128)}), f32[16,4,3,1024]{3,1,2,0:T(4,128)S(1)}, u32[]{:S(2)}, u32[]{:S(2)}) async-start(f32[16,4,3,1024]{3,1,2,0:T(4,128)} %fusion.100), calls=%async_computation | async-start | bytes 1572864 | tf_op jit(solution)/shard_map/all_to_all | solution.py:122
  179.6 24.2 %all-to-all-start.1 = ((f32[4,48,1024]{2,0,1:T(4,128)}), f32[4,48,1024]{2,0,1:T(4,128)S(1)}, u32[]{:S(2)}, u32[]{:S(2)}) async-start(f32[4,48,1024]{2,0,1:T(4,128)} %copy.53), calls=%async_computation.1 | async-start | bytes 1572864 | tf_op jit(solution)/shard_map/all_to_all | solution.py:126
